TPU v7x, 128 devices: a whole 4x4x4 slice. The times are simulated.
128 devices in a mesh: row: 16 (over z_hi, y, core), col: 8 (over z_lo, x).
Axes of the slice: x: 4, y: 4, z: 4 (z_hi: 2, z_lo: 2; z = z_hi * 2 + z_lo), core: 2. Of those that a mesh axis runs over, the one named last changes fastest.
Arguments:
- parent_inverse: float32 [24576, 24576], P('row', 'col'), may hold values from -6 to 6
- panel: float32 [24576, 1024], P(('col', 'row')), may hold values from -0.0390625 to 0.0390625
- saved_diag: float32 [1024, 1024], P('row', 'col'), may hold values from -6 to 6
Outputs:
- offdiag_block: float32 [24576, 1024], P(('row', 'col'))
- diag_block: float32 [1024, 1024], P('row', 'col')
All inputs are finite; a program needn't handle non-finite values.
Results may differ from a plain program's by a relative error of at most 0.00007.
Values sent between devices are 32-bit elements; how exact they have to be, the bound alone decides.
A program may use at most 128 MiB of HBM per device.

v0:
```python
import jax
import jax.numpy as jnp
from jax import lax
from jax.sharding import PartitionSpec as P


def spread(block, axis, holder):
    block = jnp.where(lax.axis_index(axis) == holder, block, jnp.zeros_like(block))
    return lax.psum(block, axis)


def shards(parent_inverse, panel, saved_diag):
    block_rows = parent_inverse.shape[0]
    column_count = lax.axis_size("col")
    keep_rows = block_rows // column_count
    column_panel = lax.all_gather(panel, "row", axis=0, tiled=True)
    row_index = lax.axis_index("row")
    column_index = lax.axis_index("col")
    local_half = lax.dynamic_slice_in_dim(column_panel, row_index % 2 * block_rows, block_rows, 0)
    product = lax.psum_scatter(
        jnp.dot(
            parent_inverse,
            column_panel,
            precision=lax.Precision.HIGHEST,
            preferred_element_type=jnp.float32,
        ),
        "col",
        scatter_dimension=0,
        tiled=True,
    )
    panel_half = spread(local_half, "col", row_index // 2)
    own_rows = lax.dynamic_slice_in_dim(panel_half, column_index * keep_rows, keep_rows, 0)
    offdiag_block = -product
    partial_value = lax.dot_general(
        own_rows,
        product,
        (((0,), (0,)), ((), ())),
        precision=lax.Precision.HIGHEST,
        preferred_element_type=jnp.float32,
    )
    by_columns = lax.psum_scatter(partial_value, "col", scatter_dimension=1, tiled=True)
    summed = lax.psum_scatter(by_columns, "row", scatter_dimension=0, tiled=True)
    diag_block = saved_diag + summed
    return (offdiag_block, diag_block)


def solution(mesh):
    in_specs = (P("row", "col"), P(("col", "row"), None), P("row", "col"))
    out_specs = (P(("row", "col"), None), P("row", "col"))
    return jax.shard_map(shards, mesh=mesh, in_specs=in_specs, out_specs=out_specs, check_vma=False)
```

profile of v0, /device:TPU:0, one launch (start us, length us, event | category | flops | bytes accessed | tf_op | source)
XLA Modules:
  0.0 462.0 jit_solution(5138972015593387433)
XLA Ops:
  7.2 0.0 all-gather.2.cloned.1.call-start
  7.2 0.7 all-gather.2.cloned.1.call-update
  7.9 0.0 all-reduce.2.cloned.1.call-start
  8.0 95.5 %all-gather.2.cloned.1.call-done = f32[3072,1024]{1,0:T(8,128)} async-done(((f32[192,1024]{1,0:T(8,128)}), f32[3072,1024]{1,0:T(8,128)}) %all-gather.2.cloned.1.call-update) | async-done | bytes 12582928 | tf_op jit(solution)/shard_map/all_gather | solution.py:16
  103.4 6.8 %dynamic-slice_select_fusion = f32[1536,1024]{1,0:T(8,128)} fusion(f32[3072,1024]{1,0:T(8,128)} %all-gather.2.cloned.1.call-done, s32[]{:T(128)S(6)} %select_n.28, pred[]{:T(512)S(6)} %eq.5), kind=kLoop, calls=%fused_computation | loop fusion | flops 1572864 | bytes 12582917 | tf_op jit(solution)/shard_map/jit(_where)/select_n | solution.py:8
  110.2 0.0 all-reduce.2.cloned.1.call-update
  110.2 0.0 reduce-scatter.4.cloned.1.call-start
  110.3 66.9 %fusion.3 = f32[1536,1024]{1,0:T(8,128)} fusion(f32[1536,3072]{1,0:T(8,128)} %param.3, f32[3072,1024]{1,0:T(8,128)} %all-gather.2.cloned.1.call-done), kind=kOutput, calls=%fused_computation.4 | convolution fusion | flops 57982058496 | bytes 37748736 | tf_op jit(solution)/shard_map/dot_general | solution.py:21
  177.2 0.0 reduce-scatter.4.cloned.1.call-update
  177.2 0.0 copy-start.1
  177.2 0.2 reduce-scatter.6.cloned.1.call-start
  177.5 75.2 %all-reduce.2.cloned.1.call-done = f32[1536,1024]{1,0:T(8,128)} async-done(((f32[1536,1024]{1,0:T(8,128)}), f32[1536,1024]{1,0:T(8,128)}) %all-reduce.2.cloned.1.call-update) | async-done | bytes 6291472 | tf_op jit(solution)/shard_map/psum | solution.py:9
  252.7 74.2 %reduce-scatter.4.cloned.1.call-done = f32[192,1024]{1,0:T(8,128)} async-done(((f32[1536,1024]{1,0:T(8,128)}), f32[192,1024]{1,0:T(8,128)}) %reduce-scatter.4.cloned.1.call-update) | async-done | bytes 786448 | tf_op jit(solution)/shard_map/reduce_scatter | solution.py:20
  326.9 0.0 copy-start
  326.9 6.9 %fusion = f32[1024,1024]{1,0:T(8,128)} fusion(f32[192,1024]{1,0:T(8,128)} %reduce-scatter.4.cloned.1.call-done, f32[1536,1024]{1,0:T(8,128)} %all-reduce.2.cloned.1.call-done, s32[]{:T(128)S(6)} %select_n.30), kind=kOutput, calls=%fused_computation.1 | convolution fusion | flops 2415919104 | bytes 5767172 | tf_op jit(solution)/shard_map/dot_general | solution.py:34
  333.8 0.0 reduce-scatter.6.cloned.1.call-update
  333.8 0.0 reduce-scatter.8.cloned.1.call-start
  333.9 52.0 %reduce-scatter.6.cloned.1.call-done = f32[1024,128]{1,0:T(8,128)} async-done(((f32[1024,1024]{1,0:T(8,128)}), f32[1024,128]{1,0:T(8,128)}) %reduce-scatter.6.cloned.1.call-update) | async-done | bytes 524304 | tf_op jit(solution)/shard_map/reduce_scatter | solution.py:41
  385.9 0.0 reduce-scatter.8.cloned.1.call-update
  385.9 0.0 copy-done
  385.9 0.9 neg.3
  386.9 67.3 %reduce-scatter.8.cloned.1.call-done = f32[64,128]{1,0:T(8,128)} async-done(((f32[1024,128]{1,0:T(8,128)}), f32[64,128]{1,0:T(8,128)}) %reduce-scatter.8.cloned.1.call-update) | async-done | bytes 32784 | tf_op jit(solution)/shard_map/reduce_scatter | solution.py:42
  454.1 0.0 copy-done.1
  454.1 1.4 add.25
Async XLA Ops:
  7.2 96.3 %all-gather.2.cloned.1.call-start = ((), (), s32[]{:S(2)}) async-start(), calls=%async_computation.3 | async-start | bytes 13369344 | tf_op jit(solution)/shard_map/all_gather | solution.py:16
  7.9 244.8 %all-reduce.2.cloned.1.call-start = ((), (), s32[]{:S(2)}) async-start(), calls=%async_computation.5 | async-start | bytes 12582912 | tf_op jit(solution)/shard_map/psum | solution.py:9
  110.2 216.7 %reduce-scatter.4.cloned.1.call-start = ((), (), s32[]{:S(2)}) async-start(), calls=%async_computation.4 | async-start | bytes 7077888 | tf_op jit(solution)/shard_map/reduce_scatter | solution.py:20
  177.2 276.9 %copy-start.1 = (f32[64,128]{1,0:T(8,128)S(1)}, f32[64,128]{1,0:T(8,128)}, u32[]{:S(2)}) copy-start(f32[64,128]{1,0:T(8,128)} %param.5) | copy-start | bytes 98308
  177.2 208.7 %reduce-scatter.6.cloned.1.call-start = ((), (), s32[]{:S(2)}) async-start(), calls=%async_computation.6 | async-start | bytes 4718592 | tf_op jit(solution)/shard_map/reduce_scatter | solution.py:41
  326.9 59.0 %copy-start = (f32[192,1024]{1,0:T(8,128)S(1)}, f32[192,1024]{1,0:T(8,128)}, u32[]{:S(2)}) copy-start(f32[192,1024]{1,0:T(8,128)} %reduce-scatter.4.cloned.1.call-done) | copy-start | bytes 2359300
  333.8 120.3 %reduce-scatter.8.cloned.1.call-start = ((), (), s32[]{:S(2)}) async-start(), calls=%async_computation.7 | async-start | bytes 557056 | tf_op jit(solution)/shard_map/reduce_scatter | solution.py:42
Sparse Core Ops, SparseCore 0:
  10.4 92.9 all-gather.1
  110.3 142.3 all-reduce.1
  255.1 71.7 reduce-scatter.3
  334.0 51.8 reduce-scatter.5
  389.5 64.5 reduce-scatter.7
where the time goes:
time: 462 us
  waiting for transfers between devices  365 us (79%)
  matrix products  73.8 us (16%)
  between operations  13.8 us (3%)
  other arithmetic  9.07 us (2%)
    all_gather x1, waiting for transfers between devices, shards(): column_panel = lax.all_gather(panel, 'row', axis=0, tiled=True)  95.5 us
    psum x1, waiting for transfers between devices, spread(): return lax.psum(block, axis)  75.2 us
    reduce_scatter x1, waiting for transfers between devices, shards(): lax.psum_scatter(jnp.dot(parent_inverse, column_panel, precision=lax.Prec...  74.2 us
    reduce_scatter x1, waiting for transfers between devices, shards(): lax.psum_scatter(by_columns, 'row', scatter_dimension=0, tiled=True)  67.3 us
    dot_general x1, matrix products, shards(): jnp.dot(parent_inverse, column_panel, precision=lax.Precision.HIGHEST, pr...  66.9 us
    reduce_scatter x1, waiting for transfers between devices, shards(): lax.psum_scatter(partial_value, 'col', scatter_dimension=1, tiled=True)  52 us
  transfers between devices with their start and end apart: 5, of which 5 were waited for; matrix products, arithmetic and copies ran while one was open for 15% of the time, Pallas kernels for 0%

commit v1 on v0

--- a/solution.py
+++ b/solution.py
@@ -4,9 +4,15 @@
 from jax.sharding import PartitionSpec as P
 
 
+def add_all(x, mesh_axis):
+    parts = lax.all_gather(x, mesh_axis, axis=0, tiled=False)
+    total = parts.sum(axis=0)
+    return total
+
+
 def spread(block, axis, holder):
     block = jnp.where(lax.axis_index(axis) == holder, block, jnp.zeros_like(block))
-    return lax.psum(block, axis)
+    return add_all(block, axis)
 
 
 def shards(parent_inverse, panel, saved_diag):

time: 462 us -> 803 us (1.74)
  waiting for transfers between devices: 365 us -> 684 us
  other arithmetic: 9.07 us -> 30.6 us
    all_gather x0 -> x1, waiting for transfers between devices: none -> 416 us  [add_all(): parts = lax.all_gather(x, mesh_axis, axis=0, tiled=False)]
    psum x1 -> x0, waiting for transfers between devices: 75.2 us -> none  [spread(): return lax.psum(block, axis)]
    reduce_scatter x1, waiting for transfers between devices: 74.2 us -> 52.6 us  [shards(): lax.psum_scatter(jnp.dot(parent_inverse, column_panel, precision=lax.Prec...]
    reduce_sum x0 -> x1, other arithmetic: none -> 21.5 us  [add_all(): total = parts.sum(axis=0)]
  transfers between devices with their start and end apart: 5 -> 5, of which waited for: 5 -> 5; matrix products, arithmetic and copies ran while one was open for 15% -> 11% of each run, Pallas kernels for 0% -> 0%
where the time goes in v1:
time: 803 us; the launch traced here: 802 us
  waiting for transfers between devices  684 us (85%)
  matrix products  73.7 us (9%)
  other arithmetic  30.6 us (4%)
  between operations  13.8 us (2%)
    all_gather x1, waiting for transfers between devices, add_all(): parts = lax.all_gather(x, mesh_axis, axis=0, tiled=False)  416 us
    all_gather x1, waiting for transfers between devices, shards(): column_panel = lax.all_gather(panel, 'row', axis=0, tiled=True)  95.5 us
    reduce_scatter x1, waiting for transfers between devices, shards(): lax.psum_scatter(by_columns, 'row', scatter_dimension=0, tiled=True)  67.3 us
    dot_general x1, matrix products, shards(): jnp.dot(parent_inverse, column_panel, precision=lax.Precision.HIGHEST, pr...  66.8 us
    reduce_scatter x1, waiting for transfers between devices, shards(): lax.psum_scatter(jnp.dot(parent_inverse, column_panel, precision=lax.Prec...  52.6 us
    reduce_scatter x1, waiting for transfers between devices, shards(): lax.psum_scatter(partial_value, 'col', scatter_dimension=1, tiled=True)  52 us
    reduce_sum x1, other arithmetic, add_all(): total = parts.sum(axis=0)  21.5 us
  transfers between devices with their start and end apart: 5, of which 5 were waited for; matrix products, arithmetic and copies ran while one was open for 11% of the time, Pallas kernels for 0%

profile of v1, /device:TPU:0, one launch (start us, length us, event | category | flops | bytes accessed | tf_op | source)
XLA Modules:
  0.0 802.2 jit_solution(12178304950509651453)
XLA Ops:
  7.2 0.0 all-gather.4.cloned.1.call-start
  7.2 0.7 all-gather.4.cloned.1.call-update
  7.9 0.0 all-gather.6.cloned.1.call-start
  8.0 95.5 %all-gather.4.cloned.1.call-done = f32[3072,1024]{1,0:T(8,128)} async-done(((f32[192,1024]{1,0:T(8,128)}), f32[3072,1024]{1,0:T(8,128)}) %all-gather.4.cloned.1.call-update) | async-done | bytes 12582928 | tf_op jit(solution)/shard_map/all_gather | solution.py:22
  103.4 6.7 dynamic-slice_select_fusion
  110.2 0.0 all-gather.6.cloned.1.call-update
  110.2 0.0 reduce-scatter.4.cloned.1.call-start
  110.3 66.8 %fusion.3 = f32[1536,1024]{1,0:T(8,128)} fusion(f32[1536,3072]{1,0:T(8,128)} %param.3, f32[3072,1024]{1,0:T(8,128)} %all-gather.4.cloned.1.call-done), kind=kOutput, calls=%fused_computation.4 | convolution fusion | flops 57982058496 | bytes 37748736 | tf_op jit(solution)/shard_map/dot_general | solution.py:27
  177.1 0.0 reduce-scatter.4.cloned.1.call-update
  177.1 0.2 reduce-scatter.6.cloned.1.call-start
  177.3 415.7 %all-gather.6.cloned.1.call-done = f32[12288,1024]{1,0:T(8,128)} async-done(((f32[1536,1024]{1,0:T(8,128)}), f32[12288,1024]{1,0:T(8,128)}) %all-gather.6.cloned.1.call-update) | async-done | bytes 50331664 | tf_op jit(solution)/shard_map/all_gather | solution.py:8
  593.0 21.5 %reduce_sum.9 = f32[1536,1024]{1,0:T(8,128)} reduce(f32[8,1536,1024]{2,1,0:T(8,128)} %bitcast.4, f32[]{:T(128)} %constant.41.clone.1), dimensions={0}, to_apply=%region_1.2 | reduce | flops 11010048 | bytes 56623108 | tf_op jit(solution)/shard_map/reduce_sum | solution.py:9
  614.5 0.0 copy-start.1
  614.5 52.6 %reduce-scatter.4.cloned.1.call-done = f32[192,1024]{1,0:T(8,128)} async-done(((f32[1536,1024]{1,0:T(8,128)}), f32[192,1024]{1,0:T(8,128)}) %reduce-scatter.4.cloned.1.call-update) | async-done | bytes 786448 | tf_op jit(solution)/shard_map/reduce_scatter | solution.py:26
  667.1 0.0 copy-start
  667.1 6.9 fusion
  674.0 0.0 reduce-scatter.6.cloned.1.call-update
  674.0 0.0 reduce-scatter.8.cloned.1.call-start
  674.1 52.0 %reduce-scatter.6.cloned.1.call-done = f32[1024,128]{1,0:T(8,128)} async-done(((f32[1024,1024]{1,0:T(8,128)}), f32[1024,128]{1,0:T(8,128)}) %reduce-scatter.6.cloned.1.call-update) | async-done | bytes 524304 | tf_op jit(solution)/shard_map/reduce_scatter | solution.py:47
  726.1 0.0 reduce-scatter.8.cloned.1.call-update
  726.1 0.0 copy-done
  726.1 0.9 neg.3
  727.0 67.3 %reduce-scatter.8.cloned.1.call-done = f32[64,128]{1,0:T(8,128)} async-done(((f32[1024,128]{1,0:T(8,128)}), f32[64,128]{1,0:T(8,128)}) %reduce-scatter.8.cloned.1.call-update) | async-done | bytes 32784 | tf_op jit(solution)/shard_map/reduce_scatter | solution.py:48
  794.3 0.0 copy-done.1
  794.3 1.4 add.23
Async XLA Ops:
  7.2 96.3 %all-gather.4.cloned.1.call-start = ((), (), s32[]{:S(2)}) async-start(), calls=%async_computation.3 | async-start | bytes 13369344 | tf_op jit(solution)/shard_map/all_gather | solution.py:22
  7.9 585.1 %all-gather.6.cloned.1.call-start = ((), (), s32[]{:S(2)}) async-start(), calls=%async_computation.7 | async-start | bytes 56623104 | tf_op jit(solution)/shard_map/all_gather | solution.py:8
  110.2 556.9 %reduce-scatter.4.cloned.1.call-start = ((), (), s32[]{:S(2)}) async-start(), calls=%async_computation.4 | async-start | bytes 7077888 | tf_op jit(solution)/shard_map/reduce_scatter | solution.py:26
  177.1 549.0 %reduce-scatter.6.cloned.1.call-start = ((), (), s32[]{:S(2)}) async-start(), calls=%async_computation.5 | async-start | bytes 4718592 | tf_op jit(solution)/shard_map/reduce_scatter | solution.py:47
  614.5 179.8 %copy-start.1 = (f32[64,128]{1,0:T(8,128)S(1)}, f32[64,128]{1,0:T(8,128)}, u32[]{:S(2)}) copy-start(f32[64,128]{1,0:T(8,128)} %param.5) | copy-start | bytes 98308
  667.1 59.0 %copy-start = (f32[192,1024]{1,0:T(8,128)S(1)}, f32[192,1024]{1,0:T(8,128)}, u32[]{:S(2)}) copy-start(f32[192,1024]{1,0:T(8,128)} %reduce-scatter.4.cloned.1.call-done) | copy-start | bytes 2359300
  674.0 120.3 %reduce-scatter.8.cloned.1.call-start = ((), (), s32[]{:S(2)}) async-start(), calls=%async_computation.6 | async-start | bytes 557056 | tf_op jit(solution)/shard_map/reduce_scatter | solution.py:48
Sparse Core Ops, SparseCore 0:
  10.4 92.9 all-gather.3
  110.3 482.6 all-gather.5
  595.4 71.6 reduce-scatter.3
  674.1 51.8 reduce-scatter.5
  729.7 64.5 reduce-scatter.7

commit v2 on v0

--- a/solution.py
+++ b/solution.py
@@ -13,7 +13,8 @@
     block_rows = parent_inverse.shape[0]
     column_count = lax.axis_size("col")
     keep_rows = block_rows // column_count
-    column_panel = lax.all_gather(panel, "row", axis=0, tiled=True)
+    far_arr = jnp.stack([panel for _ in range(lax.axis_size("row"))])
+    column_panel = jnp.concatenate(lax.all_to_all(far_arr, "row", 0, 0), axis=0)
     row_index = lax.axis_index("row")
     column_index = lax.axis_index("col")
     local_half = lax.dynamic_slice_in_dim(column_panel, row_index % 2 * block_rows, block_rows, 0)

time: 462 us -> 553 us (1.20)
  waiting for transfers between devices: 365 us -> 441 us
  starting transfers between devices: 0.38 us -> 8.39 us
  local copies, waits for them, and re-layouts: 0.01 us -> 7.22 us
    all_to_all x0 -> x1, waiting for transfers between devices: none -> 169 us  [shards(): column_panel = jnp.concatenate(lax.all_to_all(far_arr, 'row', 0, 0), axis=0)]
    all_gather x1 -> x0, waiting for transfers between devices: 95.5 us -> none  [shards(): column_panel = lax.all_gather(panel, 'row', axis=0, tiled=True)]
    all_to_all x0 -> x1, starting transfers between devices: none -> 8.04 us  [shards(): column_panel = jnp.concatenate(lax.all_to_all(far_arr, 'row', 0, 0), axis=0)]
    another operation x0 -> x1, local copies, waits for them, and re-layouts: none -> 7.21 us  [shards(): far_arr = jnp.stack([panel for _ in range(lax.axis_size('row'))])]
  transfers between devices with their start and end apart: 5 -> 5, of which waited for: 5 -> 5; matrix products, arithmetic and copies ran while one was open for 15% -> 12% of each run, Pallas kernels for 0% -> 0%
where the time goes in v2:
time: 553 us
  waiting for transfers between devices  441 us (80%)
  matrix products  73.8 us (13%)
  between operations  13.8 us (2%)
  other arithmetic  9.05 us (2%)
  starting transfers between devices  8.39 us (2%)
  local copies, waits for them, and re-layouts  7.22 us (1%)
    all_to_all x1, waiting for transfers between devices, shards(): column_panel = jnp.concatenate(lax.all_to_all(far_arr, 'row', 0, 0), axis=0)  169 us
    psum x1, waiting for transfers between devices, spread(): return lax.psum(block, axis)  78.4 us
    reduce_scatter x1, waiting for transfers between devices, shards(): lax.psum_scatter(jnp.dot(parent_inverse, column_panel, precision=lax.Prec...  74.2 us
    reduce_scatter x1, waiting for transfers between devices, shards(): lax.psum_scatter(by_columns, 'row', scatter_dimension=0, tiled=True)  67.3 us
    dot_general x1, matrix products, shards(): jnp.dot(parent_inverse, column_panel, precision=lax.Precision.HIGHEST, pr...  66.9 us
    reduce_scatter x1, waiting for transfers between devices, shards(): lax.psum_scatter(partial_value, 'col', scatter_dimension=1, tiled=True)  52 us
  transfers between devices with their start and end apart: 5, of which 5 were waited for; matrix products, arithmetic and copies ran while one was open for 12% of the time, Pallas kernels for 0%

profile of v2, /device:TPU:0, one launch (start us, length us, event | category | flops | bytes accessed | tf_op | source)
XLA Modules:
  0.0 553.0 jit_solution(13162477384150216974)
XLA Ops:
  7.2 7.2 %stack.2 = f32[16,192,1024]{2,1,0:T(8,128)} broadcast(f32[192,1024]{1,0:T(8,128)} %param.4), dimensions={1,2} | broadcast | bytes 13369344 | tf_op jit(solution)/shard_map/stack | solution.py:16
  14.4 8.0 %all-to-all-start = ((f32[16,192,1024]{2,1,0:T(8,128)}), f32[16,192,1024]{2,1,0:T(8,128)}, u32[]{:S(2)}, u32[]{:S(2)}) async-start(f32[16,192,1024]{2,1,0:T(8,128)} %stack.2), calls=%async_computation | async-start | bytes 25165824 | tf_op jit(solution)/shard_map/all_to_all | solution.py:17
  22.4 0.0 all-reduce.2.cloned.1.call-start
  22.5 168.8 %all-to-all-done = f32[16,192,1024]{2,1,0:T(8,128)} async-done(((f32[16,192,1024]{2,1,0:T(8,128)}), f32[16,192,1024]{2,1,0:T(8,128)}, u32[]{:S(2)}, u32[]{:S(2)}) %all-to-all-start) | async-done | bytes 12582944 | tf_op jit(solution)/shard_map/all_to_all | solution.py:17
  191.3 6.7 %dynamic-slice_select_fusion = f32[1536,1024]{1,0:T(8,128)} fusion(f32[3072,1024]{1,0:T(8,128)} %bitcast, s32[]{:T(128)S(6)} %select_n.28, pred[]{:T(512)S(6)} %eq.5), kind=kLoop, calls=%fused_computation | loop fusion | flops 1572864 | bytes 12582917 | tf_op jit(solution)/shard_map/jit(_where)/select_n | solution.py:8
  198.0 0.0 all-reduce.2.cloned.1.call-update
  198.0 0.0 reduce-scatter.4.cloned.1.call-start
  198.1 66.9 %fusion.3 = f32[1536,1024]{1,0:T(8,128)} fusion(f32[1536,3072]{1,0:T(8,128)} %param.3, f32[3072,1024]{1,0:T(8,128)} %bitcast), kind=kOutput, calls=%fused_computation.4 | convolution fusion | flops 57982058496 | bytes 37748736 | tf_op jit(solution)/shard_map/dot_general | solution.py:22
  265.0 0.0 reduce-scatter.4.cloned.1.call-update
  265.0 0.0 copy-start.1
  265.1 0.2 reduce-scatter.6.cloned.1.call-start
  265.3 78.4 %all-reduce.2.cloned.1.call-done = f32[1536,1024]{1,0:T(8,128)} async-done(((f32[1536,1024]{1,0:T(8,128)}), f32[1536,1024]{1,0:T(8,128)}) %all-reduce.2.cloned.1.call-update) | async-done | bytes 6291472 | tf_op jit(solution)/shard_map/psum | solution.py:9
  343.7 74.2 %reduce-scatter.4.cloned.1.call-done = f32[192,1024]{1,0:T(8,128)} async-done(((f32[1536,1024]{1,0:T(8,128)}), f32[192,1024]{1,0:T(8,128)}) %reduce-scatter.4.cloned.1.call-update) | async-done | bytes 786448 | tf_op jit(solution)/shard_map/reduce_scatter | solution.py:21
  417.9 0.0 copy-start
  417.9 6.9 %fusion = f32[1024,1024]{1,0:T(8,128)} fusion(f32[192,1024]{1,0:T(8,128)} %reduce-scatter.4.cloned.1.call-done, f32[1536,1024]{1,0:T(8,128)} %all-reduce.2.cloned.1.call-done, s32[]{:T(128)S(6)} %select_n.30), kind=kOutput, calls=%fused_computation.1 | convolution fusion | flops 2415919104 | bytes 5767172 | tf_op jit(solution)/shard_map/dot_general | solution.py:35
  424.8 0.0 reduce-scatter.6.cloned.1.call-update
  424.8 0.0 reduce-scatter.8.cloned.1.call-start
  424.9 52.0 %reduce-scatter.6.cloned.1.call-done = f32[1024,128]{1,0:T(8,128)} async-done(((f32[1024,1024]{1,0:T(8,128)}), f32[1024,128]{1,0:T(8,128)}) %reduce-scatter.6.cloned.1.call-update) | async-done | bytes 524304 | tf_op jit(solution)/shard_map/reduce_scatter | solution.py:42
  476.9 0.0 reduce-scatter.8.cloned.1.call-update
  476.9 0.0 copy-done
  476.9 0.9 neg.3
  477.8 67.3 %reduce-scatter.8.cloned.1.call-done = f32[64,128]{1,0:T(8,128)} async-done(((f32[1024,128]{1,0:T(8,128)}), f32[64,128]{1,0:T(8,128)}) %reduce-scatter.8.cloned.1.call-update) | async-done | bytes 32784 | tf_op jit(solution)/shard_map/reduce_scatter | solution.py:43
  545.1 0.0 copy-done.1
  545.1 1.4 add.25
Async XLA Ops:
  14.4 176.9 %all-to-all-start = ((f32[16,192,1024]{2,1,0:T(8,128)}), f32[16,192,1024]{2,1,0:T(8,128)}, u32[]{:S(2)}, u32[]{:S(2)}) async-start(f32[16,192,1024]{2,1,0:T(8,128)} %stack.2), calls=%async_computation | async-start | bytes 25165824 | tf_op jit(solution)/shard_map/all_to_all | solution.py:17
  22.4 321.3 %all-reduce.2.cloned.1.call-start = ((), (), s32[]{:S(2)}) async-start(), calls=%async_computation.5 | async-start | bytes 12582912 | tf_op jit(solution)/shard_map/psum | solution.py:9
  198.0 219.9 %reduce-scatter.4.cloned.1.call-start = ((), (), s32[]{:S(2)}) async-start(), calls=%async_computation.4 | async-start | bytes 7077888 | tf_op jit(solution)/shard_map/reduce_scatter | solution.py:21
  265.0 280.1 %copy-start.1 = (f32[64,128]{1,0:T(8,128)S(1)}, f32[64,128]{1,0:T(8,128)}, u32[]{:S(2)}) copy-start(f32[64,128]{1,0:T(8,128)} %param.5) | copy-start | bytes 98308
  265.1 211.8 %reduce-scatter.6.cloned.1.call-start = ((), (), s32[]{:S(2)}) async-start(), calls=%async_computation.6 | async-start | bytes 4718592 | tf_op jit(solution)/shard_map/reduce_scatter | solution.py:42
  417.9 58.9 %copy-start = (f32[192,1024]{1,0:T(8,128)S(1)}, f32[192,1024]{1,0:T(8,128)}, u32[]{:S(2)}) copy-start(f32[192,1024]{1,0:T(8,128)} %reduce-scatter.4.cloned.1.call-done) | copy-start | bytes 2359300
  424.8 120.3 %reduce-scatter.8.cloned.1.call-start = ((), (), s32[]{:S(2)}) async-start(), calls=%async_computation.7 | async-start | bytes 557056 | tf_op jit(solution)/shard_map/reduce_scatter | solution.py:43
Sparse Core Ops, SparseCore 0:
  198.2 145.4 all-reduce.1
  346.1 71.7 reduce-scatter.3
  425.0 51.8 reduce-scatter.5
  480.5 64.6 reduce-scatter.7
